TPU v7x, 128 devices: a whole 4x4x4 slice. The times are simulated.
128 devices in a mesh: pool: 4 (over y), seq: 32 (over x, z, core).
Axes of the slice: x: 4, y: 4, z: 4, core: 2. Of those that a mesh axis runs over, the one named last changes fastest.
Arguments:
- pool_kv: bfloat16 [16, 4096, 1024], P('pool', 'seq'), may hold values from -4 to 4
- span_home: int32 [12], replicated, may hold values from 0 to 15, as said below
- span_order: int32 [4, 3], P('pool'), may hold values from 0 to 11, as said below
- chosen: int32 [4, 14], P('pool'), may hold values from 0 to 95, as said below
- fresh_q: bfloat16 [4, 1792, 6144], P('pool', 'seq'), may hold values from -300 to 300
- fresh_kv: bfloat16 [4, 1792, 1024], P('pool', 'seq'), may hold values from -5 to 5
Outputs:
- attended: bfloat16 [4, 1792, 6144], P('pool', 'seq')
- decode_kv: bfloat16 [4, 32, 4, 96, 1024], P('pool', 'seq')
Inputs may be any that keep to these rules, and one draw needn't show every extreme that they name: `span_home`: all entries differ; home // 4 is the replica of a passage, and the 3 passages r * 3 to r * 3 + 2 of request r lie on different replicas; some replica holds a passage of every request. `span_order`: row r orders the passages r * 3 to r * 3 + 2. `chosen`: each row lists 14 different blocks in rising order; block k holds positions k * 128 to k * 128 + 127.
All inputs are finite; a program needn't handle non-finite values.
Results may differ from a plain program's by a relative error of at most 0.0035.
Values may be sent and summed in bfloat16 or wider, within the bound.
A program may use at most 192 MiB of HBM per device.

v0:
```python
import math
import jax
import jax.numpy as jnp
from jax import lax
from jax.sharding import PartitionSpec as P

KV_HEADS = 4
HEAD_DIM = 128
masked_low = -1e30


def patch_rows(values, positions, picked, fresh_all, block_len):
    block_ids = positions // block_len
    offsets = positions % block_len
    matches = block_ids[..., None] == picked
    is_fresh = jnp.any(matches, axis=-1)
    slot_ids = jnp.sum(jnp.where(matches, jnp.arange(picked.shape[0], dtype=jnp.int32), 0), axis=-1)
    source = (slot_ids * block_len + offsets).reshape(-1)
    rows_new = jnp.take(fresh_all, source, axis=0).reshape(values.shape)
    return jnp.where(is_fresh[..., None], rows_new, values)


def fold_keys(state_in, shard_piece, queries, query_pos, span_len):
    span_count, piece_rows, kv_width = shard_piece.shape
    key_pos = (
        jnp.arange(span_count, dtype=jnp.int32)[:, None] * span_len
        + jnp.arange(piece_rows, dtype=jnp.int32)[None, :]
    )
    kv_heads, query_rows, head_dim = queries.shape
    flattened = shard_piece.reshape(span_count * piece_rows, kv_heads, 2, head_dim)
    keys_all = flattened[:, :, 0]
    values_all = flattened[:, :, 1]
    pos_all = key_pos.reshape(-1)
    key_count = span_count * piece_rows
    step_len = math.gcd(key_count, 512)
    inv_root = head_dim ** (-0.5)

    def one_block(state_now, turn_at):
        running_max, total_weight, weighted = state_now
        first_key = turn_at * step_len
        key_blk = lax.dynamic_slice_in_dim(keys_all, first_key, step_len, 0)
        value_blk = lax.dynamic_slice_in_dim(values_all, first_key, step_len, 0)
        pos_blk = lax.dynamic_slice_in_dim(pos_all, first_key, step_len, 0)
        scores = (
            jnp.einsum("hqd,khd->hqk", queries, key_blk, preferred_element_type=jnp.float32)
            * inv_root
        )
        allowed = pos_blk[None, None, :] <= query_pos[None, :, None]
        scores = jnp.where(allowed, scores, masked_low)
        newest = jnp.maximum(running_max, jnp.max(scores, axis=-1))
        weights = jnp.where(allowed, jnp.exp(scores - newest[..., None]), 0.0)
        factor = jnp.exp(running_max - newest)
        total_weight = total_weight * factor + jnp.sum(weights, axis=-1)
        weighted = weighted * factor[..., None] + jnp.einsum(
            "hqk,khd->hqd",
            weights.astype(jnp.bfloat16),
            value_blk,
            preferred_element_type=jnp.float32,
        )
        return ((newest, total_weight, weighted), None)

    state_out, _ = lax.scan(one_block, state_in, jnp.arange(key_count // step_len))
    return state_out


def shards(pool_kv, span_home, span_order, chosen, fresh_q, fresh_kv):
    pool_count = lax.axis_size("pool")
    seq_count = lax.axis_size("seq")
    replica = lax.axis_index("pool")
    my_seat = lax.axis_index("seq")
    slot_count, block_len, kv_width = pool_kv.shape
    span_count = span_order.shape[1]
    span_len = block_len * seq_count
    head_dim = HEAD_DIM
    kv_heads = KV_HEADS
    picked = chosen[0]
    span_total = span_home.shape[0]
    home_replica = span_home // slot_count
    home_slot = span_home % slot_count
    span_request = jnp.arange(span_total, dtype=jnp.int32) // span_count
    requests = jnp.arange(pool_count, dtype=jnp.int32)
    held = (home_replica == replica)[None, :] & (span_request[None, :] == requests[:, None])
    in_slot = home_slot[None, :, None] == jnp.arange(slot_count, dtype=jnp.int32)[None, None, :]
    selector = jnp.any(held[:, :, None] & in_slot, axis=1).astype(jnp.bfloat16)
    outgoing = jnp.einsum(
        "rk,ktc->rtc", selector, pool_kv, preferred_element_type=jnp.float32
    ).astype(jnp.bfloat16)
    arrived = lax.all_to_all(outgoing, "pool", split_axis=0, concat_axis=0, tiled=True)
    order_row = span_order[0]
    lookup = order_row[:, None] == jnp.arange(span_total, dtype=jnp.int32)[None, :]
    source_replica = jnp.sum(jnp.where(lookup, home_replica[None, :], 0), axis=1)
    chooser = (source_replica[:, None] == requests[None, :]).astype(jnp.bfloat16)
    cached = jnp.einsum("jp,ptc->jtc", chooser, arrived, preferred_element_type=jnp.float32).astype(
        jnp.bfloat16
    )
    fresh_all = lax.all_gather(fresh_kv[0], "seq", axis=0, tiled=True)
    block_ids = jnp.arange(span_count, dtype=jnp.int32)[:, None] * seq_count + my_seat
    local_pos = block_ids * block_len + jnp.arange(block_len, dtype=jnp.int32)[None, :]
    patched = patch_rows(cached, local_pos, picked, fresh_all, block_len)
    row_count = fresh_q.shape[1]
    q_width = fresh_q.shape[2]
    group = q_width // (kv_heads * head_dim)
    list_rows = my_seat * row_count + jnp.arange(row_count, dtype=jnp.int32)
    list_block = list_rows // block_len
    base_block = jnp.sum(
        jnp.where(
            list_block[:, None] == jnp.arange(picked.shape[0], dtype=jnp.int32)[None, :],
            picked[None, :],
            0,
        ),
        axis=1,
    )
    query_pos = base_block * block_len + list_rows % block_len
    queries = fresh_q[0].reshape(row_count, kv_heads, group, head_dim).transpose(1, 2, 0, 3)
    queries = queries.reshape(kv_heads, group * row_count, head_dim)
    pos_tiled = jnp.tile(query_pos, group)
    start_state = (
        jnp.full((kv_heads, group * row_count), masked_low, jnp.float32),
        jnp.zeros((kv_heads, group * row_count), jnp.float32),
        jnp.zeros((kv_heads, group * row_count, head_dim), jnp.float32),
    )
    final_state = fold_keys(
        start_state,
        lax.all_gather(patched, "seq", axis=1, tiled=True),
        queries,
        pos_tiled,
        span_len,
    )
    running_max, total_weight, weighted = final_state
    attended = (weighted / total_weight[..., None]).reshape(kv_heads, group, row_count, head_dim)
    attended = attended.transpose(2, 0, 1, 3).reshape(1, row_count, q_width).astype(jnp.bfloat16)
    per_group = kv_heads // pool_count
    run_len = block_len // seq_count
    laid = patched.reshape(span_count, seq_count, run_len, pool_count, per_group, 2 * head_dim)
    laid = laid.transpose(3, 1, 4, 0, 2, 5).reshape(
        pool_count, seq_count, per_group, span_count, run_len * 2 * head_dim
    )
    merged = laid.reshape(pool_count * seq_count, per_group, span_count, run_len * 2 * head_dim)
    landed = lax.all_to_all(merged, ("pool", "seq"), split_axis=0, concat_axis=0, tiled=True)
    landed = landed.reshape(pool_count, seq_count, per_group, span_count, run_len * 2 * head_dim)
    decoded = landed.transpose(2, 0, 3, 1, 4).reshape(
        per_group, 1, pool_count, span_count * seq_count, run_len * 2 * head_dim
    )
    return (attended, decoded)


def solution(mesh):
    in_specs = (
        P("pool", "seq", None),
        P(),
        P("pool", None),
        P("pool", None),
        P("pool", "seq", None),
        P("pool", "seq", None),
    )
    out_specs = (P("pool", "seq", None), P("pool", "seq", None, None, None))
    return jax.shard_map(shards, mesh=mesh, in_specs=in_specs, out_specs=out_specs, check_vma=False)
```

profile of v0, /device:TPU:1, one launch (start us, length us, event | category | flops | bytes accessed | tf_op | source)
XLA Modules:
  0.0 632.1 jit_solution(8040437564425881074)
XLA Ops:
  11.7 5.0 all-to-all-start
  17.5 42.0 %all-gather.6.cloned.1.call-done = bf16[1,1792,1024]{2,1,0:T(8,128)(2,1)} async-done(((bf16[1,56,1024]{2,1,0:T(8,128)(2,1)}), bf16[1,1792,1024]{2,1,0:T(8,128)(2,1)}) %all-gather.6.cloned.1.call-update) | async-done | bytes 3670032 | tf_op jit(solution)/shard_map/all_gather | solution.py:96
  59.5 5.3 gather_fusion
  71.5 7.2 %all-to-all-start.1 = ((bf16[128,1,3,1024]{3,2,1,0:T(4,128)(2,1)}), bf16[128,1,3,1024]{3,2,1,0:T(4,128)(2,1)S(1)}, u32[]{:S(2)}, u32[]{:S(2)}) async-start(bf16[128,1,3,1024]{3,2,1,0:T(4,128)(2,1)} %reshape.349), calls=%async_computation.1 | async-start | bytes 2097152 | tf_op jit(solution)/shard_map/all_to_all | solution.py:139
  81.1 27.9 %all-to-all-done.1 = bf16[128,1,3,1024]{3,2,1,0:T(4,128)(2,1)S(1)} async-done(((bf16[128,1,3,1024]{3,2,1,0:T(4,128)(2,1)}), bf16[128,1,3,1024]{3,2,1,0:T(4,128)(2,1)S(1)}, u32[]{:S(2)}, u32[]{:S(2)}) %all-to-all-start.1) | async-done | bytes 786464 | tf_op jit(solution)/shard_map/all_to_all | solution.py:139
  110.2 60.9 %all-gather.4.cloned.1.call-done = bf16[3,4096,1024]{2,1,0:T(8,128)(2,1)} async-done(((bf16[3,128,1024]{2,1,0:T(8,128)(2,1)}), bf16[3,4096,1024]{2,1,0:T(8,128)(2,1)}) %all-gather.4.cloned.1.call-update) | async-done | bytes 25165840 | tf_op jit(solution)/shard_map/all_gather | solution.py:124
  171.1 40.5 %reshape.332 = bf16[12288,4,2,128]{3,2,1,0:T(2,128)(2,1)} reshape(bf16[3,4096,1024]{2,1,0:T(8,128)(2,1)} %all-gather.4.cloned.1.call-done) | data formatting | bytes 50331648 | tf_op jit(solution)/shard_map/reshape | solution.py:30
  211.6 47.1 %fusion.38 = (bf16[12288,4,1,128]{3,2,1,0:T(2,128)(2,1)}, bf16[12288,4,1,128]{3,2,1,0:T(2,128)(2,1)}) fusion(bf16[12288,4,2,128]{3,2,1,0:T(2,128)(2,1)} %reshape.332), kind=kLoop, calls=%fused_computation.93 | loop fusion | bytes 50331648 | tf_op jit(solution)/shard_map/slice | solution.py:32
  258.7 27.3 %copy_bitcast_fusion = (bf16[12288,4,128]{2,0,1:T(8,128)(2,1)}, bf16[12288,4,128]{2,0,1:T(8,128)(2,1)}) fusion(bf16[12288,4,1,128]{3,2,1,0:T(2,128)(2,1)} %get-tuple-element.129, bf16[12288,4,1,128]{3,2,1,0:T(2,128)(2,1)} %get-tuple-element.130), kind=kLoop, calls=%fused_computation.24 | loop fusion | bytes 50331648 | tf_op jit(solution)/shard_map/squeeze | solution.py:32
  286.1 337.2 %while.15 = (s32[]{:T(128)}, f32[4,672]{1,0:T(4,128)S(1)}, f32[4,672]{1,0:T(4,128)S(1)}, f32[4,672,128]{2,1,0:T(8,128)S(1)}, s32[24]{0:T(128)S(1)}, /*index=5*/s...) while((s32[]{:T(128)}, f32[4,672]{1,0:T(4,128)S(1)}, ...), condition=%wide.region_8.9_spmd.clone, body=%wide.region_5.8_spmd.clone.sunk | while | flops 723924096 | bytes 44590032 | solution.py:62
  287.9 4.5 fusion.50
  292.4 4.4 fusion.51
  301.9 4.5 fusion.50
  306.4 4.4 fusion.51
  316.0 4.5 fusion.50
  320.5 4.4 fusion.51
  330.0 4.5 fusion.50
  334.5 4.4 fusion.51
  344.1 4.5 fusion.50
  358.1 4.5 fusion.50
  362.6 4.4 fusion.51
  372.2 4.5 fusion.50
  376.7 4.4 fusion.51
  386.2 4.5 fusion.50
  390.7 4.4 fusion.51
  400.3 4.5 fusion.50
  404.8 4.4 fusion.51
  414.3 4.5 fusion.50
  418.8 4.4 fusion.51
  428.4 4.5 fusion.50
  442.4 4.5 fusion.50
  446.9 4.4 fusion.51
  456.5 4.5 fusion.50
  461.0 4.4 fusion.51
  470.5 4.5 fusion.50
  475.0 4.4 fusion.51
  484.6 4.5 fusion.50
  498.6 4.5 fusion.50
  512.7 4.5 fusion.50
  517.2 4.4 fusion.51
  526.7 4.5 fusion.50
  531.2 4.4 fusion.51
  540.8 4.5 fusion.50
  554.8 4.5 fusion.50
  568.9 4.5 fusion.50
  582.9 4.5 fusion.50
  597.0 4.5 fusion.50
  611.0 4.5 fusion.50
  (331 shorter events, 167.1 us)
Async XLA Ops:
  7.2 2.3 copy-start
  7.2 9.6 %copy-start.4 = (s32[1,14]{1,0:T(1,128)S(1)}, s32[1,14]{1,0:T(1,128)}, u32[]{:S(2)}) copy-start(s32[1,14]{1,0:T(1,128)} %param.11) | copy-start | bytes 172
  7.2 10.2 %copy-start.5 = (s32[1,3]{1,0:T(1,128)S(1)}, s32[1,3]{1,0:T(1,128)}, u32[]{:S(2)}) copy-start(s32[1,3]{1,0:T(1,128)} %param.10) | copy-start | bytes 40
  7.2 52.3 %all-gather.6.cloned.1.call-start = ((), (), s32[]{:S(2)}) async-start(), calls=%async_computation.3 | async-start | bytes 3784704 | tf_op jit(solution)/shard_map/all_gather | solution.py:96
  11.7 53.2 %all-to-all-start = ((bf16[4,128,1024]{2,1,0:T(8,128)(2,1)}), bf16[4,128,1024]{2,1,0:T(8,128)(2,1)S(1)}, u32[]{:S(2)}, u32[]{:S(2)}) async-start(bf16[4,128,1024]{2,1,0:T(8,128)(2,1)} %copy.49), calls=%async_computation | async-start | bytes 2097152 | tf_op jit(solution)/shard_map/all_to_all | solution.py:88
  16.6 154.5 %all-gather.4.cloned.1.call-start = ((), (), s32[]{:S(2)}) async-start(), calls=%async_computation.2 | async-start | bytes 25952256 | tf_op jit(solution)/shard_map/all_gather | solution.py:124
  71.5 37.4 %all-to-all-start.1 = ((bf16[128,1,3,1024]{3,2,1,0:T(4,128)(2,1)}), bf16[128,1,3,1024]{3,2,1,0:T(4,128)(2,1)S(1)}, u32[]{:S(2)}, u32[]{:S(2)}) async-start(bf16[128,1,3,1024]{3,2,1,0:T(4,128)(2,1)} %reshape.349), calls=%async_computation.1 | async-start | bytes 2097152 | tf_op jit(solution)/shard_map/all_to_all | solution.py:139
  258.7 27.3 %copy-start.3 = (f32[4,672,128]{2,1,0:T(8,128)S(1)}, f32[4,672,128]{2,1,0:T(8,128)}, u32[]{:S(2)}) copy-start(f32[4,672,128]{2,1,0:T(8,128)} %custom-call.2) | copy-start | bytes 4128772
  292.4 4.4 copy-start.2
  306.4 4.4 copy-start.2
  320.5 4.4 copy-start.2
  334.5 4.4 copy-start.2
  348.6 4.4 copy-start.2
  362.6 4.4 copy-start.2
  376.7 4.4 copy-start.2
  390.7 4.4 copy-start.2
  404.8 4.4 copy-start.2
  418.8 4.4 copy-start.2
  432.9 4.4 copy-start.2
  446.9 4.4 copy-start.2
  461.0 4.4 copy-start.2
  475.0 4.4 copy-start.2
  489.1 4.4 copy-start.2
  503.1 4.4 copy-start.2
  517.2 4.4 copy-start.2
  531.2 4.4 copy-start.2
  545.3 4.4 copy-start.2
  559.3 4.4 copy-start.2
  573.4 4.4 copy-start.2
  587.4 4.4 copy-start.2
  601.5 4.4 copy-start.2
  615.5 4.4 copy-start.2
  623.3 2.0 copy-start.1
Sparse Core Ops, SparseCore 0:
  10.3 49.2 all-gather.5
  69.1 102.0 all-gather.3
where the time goes:
time: 636 us; the launch traced here: 632 us
  matrix products  191 us (30%)
  local copies, waits for them, and re-layouts  150 us (24%)
  waiting for transfers between devices  131 us (21%)
  other arithmetic  114 us (18%)
  loops' own time  18.3 us (3%)
  between operations  14.3 us (2%)
  starting transfers between devices  12.2 us (2%)
    dot_general x24, matrix products, one_block(): jnp.einsum('hqd,khd->hqk', queries, key_blk, preferred_element_type=jnp.f...  108 us
    reduce_sum x24, other arithmetic, one_block(): total_weight = total_weight * factor + jnp.sum(weights, axis=-1)  105 us
    dot_general x24, matrix products, one_block(): jnp.einsum('hqk,khd->hqd', weights.astype(jnp.bfloat16), value_blk, prefe...  79.2 us
    all_gather x1, waiting for transfers between devices, shards(): lax.all_gather(patched, 'seq', axis=1, tiled=True)  60.9 us
    slice x1, local copies, waits for them, and re-layouts, fold_keys(): values_all = flattened[:, :, 1]  47.1 us
    all_gather x1, waiting for transfers between devices, shards(): fresh_all = lax.all_gather(fresh_kv[0], 'seq', axis=0, tiled=True)  42 us
    reshape x1, local copies, waits for them, and re-layouts, fold_keys(): shard_piece.reshape(span_count * piece_rows, kv_heads, 2, head_dim)  40.5 us
    all_to_all x1, waiting for transfers between devices, shards(): lax.all_to_all(merged, ('pool', 'seq'), split_axis=0, concat_axis=0, tile...  27.9 us
  transfers between devices with their start and end apart: 4, of which 3 were waited for; matrix products, arithmetic and copies ran while one was open for 3% of the time, Pallas kernels for 0%

commit v1 on v0

--- a/solution.py
+++ b/solution.py
@@ -121,7 +121,12 @@
     )
     final_state = fold_keys(
         start_state,
-        lax.all_gather(patched, "seq", axis=1, tiled=True),
+        jnp.concatenate(
+            lax.all_to_all(
+                jnp.stack([patched for _ in range(lax.psum(1, "seq"))], axis=0), "seq", 0, 0
+            ),
+            axis=1,
+        ),
         queries,
         pos_tiled,
         span_len,

time: 636 us -> 959 us (1.51)
  the two profiles are of different devices: /device:TPU:1 before, /device:TPU:36 now
where the time goes in v1:
time: 959 us; the launch traced here: 954 us
  waiting for transfers between devices  463 us (48%)
  matrix products  192 us (20%)
  local copies, waits for them, and re-layouts  129 us (13%)
  other arithmetic  114 us (12%)
  starting transfers between devices  23.1 us (2%)
  loops' own time  18.3 us (2%)
  between operations  14.3 us (1%)
    all_to_all x1, waiting for transfers between devices, shards(): lax.all_to_all(jnp.stack([patched for _ in range(lax.psum(1, 'seq'))], ax...  408 us
    dot_general x24, matrix products, one_block(): jnp.einsum('hqd,khd->hqk', queries, key_blk, preferred_element_type=jnp.f...  108 us
    reduce_sum x24, other arithmetic, one_block(): total_weight = total_weight * factor + jnp.sum(weights, axis=-1)  105 us
    dot_general x24, matrix products, one_block(): jnp.einsum('hqk,khd->hqd', weights.astype(jnp.bfloat16), value_blk, prefe...  80.7 us
    all_gather x1, waiting for transfers between devices, shards(): fresh_all = lax.all_gather(fresh_kv[0], 'seq', axis=0, tiled=True)  39 us
    another operation x1, local copies, waits for them, and re-layouts, fold_keys(): shard_piece.reshape(span_count * piece_rows, kv_heads, 2, head_dim)  35.5 us
    reshape x1, local copies, waits for them, and re-layouts, shards(): jnp.concatenate(lax.all_to_all(jnp.stack([patched for _ in range(lax.psum...  32 us
  transfers between devices with their start and end apart: 4, of which 3 were waited for; matrix products, arithmetic and copies ran while one was open for 1% of the time, Pallas kernels for 0%

profile of v1, /device:TPU:36, one launch (start us, length us, event | category | flops | bytes accessed | tf_op | source)
XLA Modules:
  0.0 953.9 jit_solution(9249702560983733456)
XLA Ops:
  11.7 4.5 all-to-all-start
  17.0 39.0 %all-gather.3.cloned.1.call-done = bf16[1,1792,1024]{2,1,0:T(8,128)(2,1)} async-done(((bf16[1,56,1024]{2,1,0:T(8,128)(2,1)}), bf16[1,1792,1024]{2,1,0:T(8,128)(2,1)}) %all-gather.3.cloned.1.call-update) | async-done | bytes 3670032 | tf_op jit(solution)/shard_map/all_gather | solution.py:96
  56.0 5.3 gather_fusion
  66.7 9.4 all-to-all-start.2
  77.3 15.0 %all-to-all-done.2 = bf16[128,1,3,1024]{3,2,1,0:T(4,128)(2,1)S(1)} async-done(((bf16[128,1,3,1024]{3,2,1,0:T(4,128)(2,1)}), bf16[128,1,3,1024]{3,2,1,0:T(4,128)(2,1)S(1)}, u32[]{:S(2)}, u32[]{:S(2)}) %all-to-all-start.2) | async-done | bytes 786464 | tf_op jit(solution)/shard_map/all_to_all | solution.py:144
  92.3 9.4 stack.2
  101.7 9.2 all-to-all-start.1
  113.4 407.9 %all-to-all-done.1 = bf16[32,3,128,1024]{3,2,1,0:T(8,128)(2,1)} async-done(((bf16[32,3,128,1024]{3,2,1,0:T(8,128)(2,1)}), bf16[32,3,128,1024]{3,2,1,0:T(8,128)(2,1)}, u32[]{:S(2)}, u32[]{:S(2)}) %all-to-all-start.1) | async-done | bytes 25165856 | tf_op jit(solution)/shard_map/all_to_all | solution.py:125
  521.3 32.0 %copy.70 = bf16[3,32,128,1024]{2,1,0,3:T(8,128)(2,1)} copy(bf16[3,32,128,1024]{3,2,0,1:T(8,128)(2,1)} %bitcast.6) | data formatting | bytes 50331648 | tf_op jit(solution)/shard_map/reshape | solution.py:124
  553.3 35.5 %reshape_reshape.6 = bf16[12288,4,2,128]{0,3,2,1:T(8,128)(2,1)} reshape(bf16[3,32,128,1024]{2,1,0,3:T(8,128)(2,1)} %copy.70) | data formatting | bytes 50331648 | tf_op jit(solution)/shard_map/reshape;reshape | solution.py:30
  588.8 17.8 %slice_bitcast_fusion = (bf16[12288,4,128]{0,2,1:T(8,128)(2,1)}, bf16[12288,4,128]{0,2,1:T(8,128)(2,1)}) fusion(bf16[12288,4,2,128]{0,3,2,1:T(8,128)(2,1)} %reshape_reshape.6), kind=kLoop, calls=%fused_computation.24 | loop fusion | bytes 50331648 | tf_op jit(solution)/shard_map/squeeze | solution.py:32
  606.7 338.3 %while.15 = (s32[]{:T(128)}, f32[4,672]{1,0:T(4,128)S(1)}, f32[4,672]{1,0:T(4,128)S(1)}, f32[4,672,128]{2,1,0:T(8,128)S(1)}, s32[24]{0:T(128)S(1)}, /*index=5*/s...) while((s32[]{:T(128)}, f32[4,672]{1,0:T(4,128)S(1)}, ...), condition=%wide.region_8.9_spmd.clone, body=%wide.region_5.8_spmd.clone.sunk | while | flops 723924096 | bytes 44590032 | solution.py:62
  608.5 4.5 fusion.49
  622.6 4.5 fusion.49
  636.7 4.5 fusion.49
  641.2 4.4 fusion.50
  650.8 4.5 fusion.49
  655.3 4.4 fusion.50
  664.9 4.5 fusion.49
  669.4 4.4 fusion.50
  679.0 4.5 fusion.49
  683.5 4.4 fusion.50
  693.1 4.5 fusion.49
  697.6 4.4 fusion.50
  707.2 4.5 fusion.49
  711.7 4.4 fusion.50
  721.3 4.5 fusion.49
  725.8 4.4 fusion.50
  735.4 4.5 fusion.49
  749.5 4.5 fusion.49
  763.6 4.5 fusion.49
  777.7 4.5 fusion.49
  782.2 4.4 fusion.50
  791.8 4.5 fusion.49
  796.3 4.4 fusion.50
  805.9 4.5 fusion.49
  810.4 4.4 fusion.50
  820.0 4.5 fusion.49
  824.5 4.4 fusion.50
  834.1 4.5 fusion.49
  838.6 4.4 fusion.50
  848.2 4.5 fusion.49
  862.3 4.5 fusion.49
  876.4 4.5 fusion.49
  890.4 4.5 fusion.49
  904.5 4.5 fusion.49
  918.6 4.5 fusion.49
  932.7 4.5 fusion.49
  (333 shorter events, 176.1 us)
Async XLA Ops:
  7.2 2.3 copy-start
  7.2 9.0 copy-start.5
  7.2 9.6 %copy-start.6 = (s32[1,3]{1,0:T(1,128)S(1)}, s32[1,3]{1,0:T(1,128)}, u32[]{:S(2)}) copy-start(s32[1,3]{1,0:T(1,128)} %param.10) | copy-start | bytes 40
  7.2 48.8 %all-gather.3.cloned.1.call-start = ((), (), s32[]{:S(2)}) async-start(), calls=%async_computation.3 | async-start | bytes 3784704 | tf_op jit(solution)/shard_map/all_gather | solution.py:96
  11.7 49.6 %all-to-all-start = ((bf16[4,128,1024]{2,1,0:T(8,128)(2,1)}), bf16[4,128,1024]{2,1,0:T(8,128)(2,1)S(1)}, u32[]{:S(2)}, u32[]{:S(2)}) async-start(bf16[4,128,1024]{2,1,0:T(8,128)(2,1)} %copy.67), calls=%async_computation | async-start | bytes 2097152 | tf_op jit(solution)/shard_map/all_to_all | solution.py:88
  66.7 25.6 %all-to-all-start.2 = ((bf16[128,1,3,1024]{3,2,1,0:T(4,128)(2,1)}), bf16[128,1,3,1024]{3,2,1,0:T(4,128)(2,1)S(1)}, u32[]{:S(2)}, u32[]{:S(2)}) async-start(bf16[128,1,3,1024]{3,2,1,0:T(4,128)(2,1)} %reshape.351), calls=%async_computation.2 | async-start | bytes 2097152 | tf_op jit(solution)/shard_map/all_to_all | solution.py:144
  101.7 9.2 copy-start.4
  101.7 419.6 %all-to-all-start.1 = ((bf16[32,3,128,1024]{3,2,1,0:T(8,128)(2,1)}), bf16[32,3,128,1024]{3,2,1,0:T(8,128)(2,1)}, u32[]{:S(2)}, u32[]{:S(2)}) async-start(bf16[32,3,128,1024]{3,2,1,0:T(8,128)(2,1)} %stack.2), calls=%async_computation.1 | async-start | bytes 50331648 | tf_op jit(solution)/shard_map/all_to_all | solution.py:125
  588.8 17.9 %copy-start.3 = (f32[4,672,128]{2,1,0:T(8,128)S(1)}, f32[4,672,128]{2,1,0:T(8,128)}, u32[]{:S(2)}) copy-start(f32[4,672,128]{2,1,0:T(8,128)} %custom-call.2) | copy-start | bytes 4128772
  613.0 4.4 copy-start.2
  627.1 4.4 copy-start.2
  641.2 4.4 copy-start.2
  655.3 4.4 copy-start.2
  669.4 4.4 copy-start.2
  683.5 4.4 copy-start.2
  697.6 4.4 copy-start.2
  711.7 4.4 copy-start.2
  725.8 4.4 copy-start.2
  739.9 4.4 copy-start.2
  754.0 4.4 copy-start.2
  768.1 4.4 copy-start.2
  782.2 4.4 copy-start.2
  796.3 4.4 copy-start.2
  810.4 4.4 copy-start.2
  824.5 4.4 copy-start.2
  838.5 4.4 copy-start.2
  852.6 4.4 copy-start.2
  866.7 4.4 copy-start.2
  880.8 4.4 copy-start.2
  894.9 4.4 copy-start.2
  909.0 4.4 copy-start.2
  923.1 4.4 copy-start.2
  937.2 4.4 copy-start.2
  945.0 2.0 copy-start.1
Sparse Core Ops, SparseCore 0:
  10.3 45.7 all-gather.2
